TPU v7x, 256 devices: a whole 4x4x8 slice. The times are simulated.
256 devices in a mesh: dp: 64 (over x, z, core), proto: 4 (over y).
Axes of the slice: x: 4, y: 4, z: 8, core: 2. Of those that a mesh axis runs over, the one named last changes fastest.
Arguments:
- embeddings: bfloat16 [65536, 1024], P(('dp', 'proto')), may hold values from -6 to 6
- centres: bfloat16 [8192, 1024], P('proto'), may hold values from -0.1875 to 0.1875
Outputs:
- updated: bfloat16 [8192, 1024], P('proto')
All inputs are finite; a program needn't handle non-finite values.
Results may differ from a plain program's by a relative error of at most 0.0074.
Values may be sent and summed in bfloat16 or wider, within the bound.
A program may use at most 64 MiB of HBM per device.

v0:
```python
import jax
import jax.numpy as jnp
from jax import lax
from jax.sharding import PartitionSpec as P

ITERS = 3


def normalise(rows):
    values = rows.astype(jnp.float32)
    scaled = values * lax.rsqrt(jnp.mean(values * values, axis=1, keepdims=True) + 1e-05)
    return scaled.astype(jnp.bfloat16)


def column_total(partial_sum):
    return lax.psum(partial_sum, "dp")


def row_total(partial_sum):
    return lax.psum(partial_sum, "proto")


def per_device(embeddings, centres):
    unit = normalise(embeddings)
    group = lax.all_gather(unit, "proto", axis=0, tiled=True)
    scores = lax.dot_general(
        group, centres, (((1,), (1,)), ((), ())), preferred_element_type=jnp.float32
    )
    plan = jnp.exp(4.0 * scores)
    total_rows = group.shape[0] * lax.axis_size("dp")
    total_cols = centres.shape[0] * lax.axis_size("proto")
    for step in range(ITERS):
        colsum = column_total(jnp.sum(plan, axis=0))
        plan = plan / (total_cols * colsum)[None, :]
        rowsum = row_total(jnp.sum(plan, axis=1))
        plan = plan / (total_rows * rowsum)[:, None]
    codes = (total_rows * plan).astype(jnp.bfloat16)
    share = lax.psum_scatter(
        lax.dot_general(codes, group, (((0,), (0,)), ((), ())), preferred_element_type=jnp.float32),
        "dp",
        scatter_dimension=0,
        tiled=True,
    )
    rescaled = share * lax.rsqrt(jnp.mean(share * share, axis=1, keepdims=True) + 1e-05)
    return lax.all_gather(rescaled.astype(jnp.bfloat16), "dp", axis=0, tiled=True)


def solution(mesh):
    return jax.shard_map(
        per_device,
        mesh=mesh,
        in_specs=(P(("dp", "proto"), None), P("proto", None)),
        out_specs=P("proto", None),
        check_vma=False,
    )
```

profile of v0, /device:TPU:1, one launch (start us, length us, event | category | flops | bytes accessed | tf_op | source)
XLA Modules:
  0.0 737.2 jit_solution(6118723697224441080)
XLA Ops:
  6.5 0.0 all-gather.3.cloned.1.call-start
  6.5 1.2 fusion.15
  7.8 2.0 fusion.16
  9.8 0.0 all-gather.3.cloned.1.call-update
  9.8 0.0 reduce-scatter.2.cloned.1.call-start
  9.8 37.1 %all-gather.3.cloned.1.call-done = bf16[1024,1024]{1,0:T(8,128)(2,1)} async-done(((bf16[256,1024]{1,0:T(8,128)(2,1)}), bf16[1024,1024]{1,0:T(8,128)(2,1)}) %all-gather.3.cloned.1.call-update) | async-done | bytes 2097168 | tf_op jit(solution)/shard_map/all_gather | solution.py:25
  46.9 10.6 %fusion.18 = (f32[2048]{0:T(1024)S(1)}, f32[1024,2048]{1,0:T(8,128)}) fusion(bf16[1024,1024]{1,0:T(8,128)(2,1)} %all-gather.3.cloned.1.call-done, bf16[2048,1024]{1,0:T(8,128)(2,1)} %param.3), kind=kOutput, calls=%fused_computation.33 | convolution fusion | flops 4299159552 | bytes 14688256 | tf_op jit(solution)/shard_map/dot_general | solution.py:26
  57.5 126.7 %psum.42 = f32[2048]{0:T(1024)S(1)} all-reduce(f32[2048]{0:T(1024)S(1)} %get-tuple-element.5), channel_id=1, replica_groups=mesh['dp'=64,'proto'=4] {'dp'}, use_global_device_ids=true, to_apply=%region_2.0 | all-reduce | flops 2048 | bytes 16384 | tf_op jit(solution)/shard_map/psum | solution.py:16
  184.3 4.0 divide_reduce_fusion
  188.3 6.6 psum.43
  194.9 4.2 fusion.8
  199.0 132.3 %psum.44 = f32[2048]{0:T(1024)S(1)} all-reduce(f32[2048]{0:T(1024)S(1)} %fusion.8), channel_id=1, replica_groups=mesh['dp'=64,'proto'=4] {'dp'}, use_global_device_ids=true, to_apply=%region_6.0 | all-reduce | flops 2048 | bytes 16384 | tf_op jit(solution)/shard_map/psum | solution.py:16
  331.4 4.4 fusion.10
  335.8 6.9 psum.45
  342.7 0.0 copy-start
  342.7 4.6 fusion.11
  347.3 128.1 %psum.46 = f32[2048]{0:T(1024)S(1)} all-reduce(f32[2048]{0:T(1024)S(1)} %fusion.11), channel_id=1, replica_groups=mesh['dp'=64,'proto'=4] {'dp'}, use_global_device_ids=true, to_apply=%region_10.0 | all-reduce | flops 2048 | bytes 16384 | tf_op jit(solution)/shard_map/psum | solution.py:16
  475.4 4.7 fusion.12
  480.1 6.6 psum.47
  486.7 0.0 copy-done
  486.7 12.4 %fusion.13 = f32[2048,1024]{1,0:T(8,128)} fusion(bf16[1024,1024]{1,0:T(8,128)(2,1)S(1)} %copy-done, f32[1024,2048]{1,0:T(8,128)} %get-tuple-element.6, f32[1024]{0:T(1024)S(1)} %broadcast_multiply_fusion.3, f32[2048]{0:T(1024)S(1)} %broadcast_multiply_fusion, f32[1024]{0:T(1024)S(1)} %broadcast_multiply_fusion.4, f32[2048]{0:T(1024)S(1)} %broadcast_multiply_fusion.1, ...), kind=kOutput, calls=%fused_computation.17 | convolution fusion | flops 4311744512 | bytes 18911232 | tf_op jit(solution)/shard_map/dot_general | solution.py:39
  499.1 0.0 reduce-scatter.2.cloned.1.call-update
  499.2 0.0 all-gather.5.cloned.1.call-start
  499.2 141.6 %reduce-scatter.2.cloned.1.call-done = f32[32,1024]{1,0:T(8,128)} async-done(((f32[2048,1024]{1,0:T(8,128)}), f32[32,1024]{1,0:T(8,128)}) %reduce-scatter.2.cloned.1.call-update) | async-done | bytes 131088 | tf_op jit(solution)/shard_map/reduce_scatter | solution.py:38
  640.8 1.0 multiply_reduce_fusion
  641.8 1.6 multiply_convert_fusion
  643.4 0.0 all-gather.5.cloned.1.call-update
  643.5 82.6 %all-gather.5.cloned.1.call-done = bf16[2048,1024]{1,0:T(8,128)(2,1)} async-done(((bf16[32,1024]{1,0:T(8,128)(2,1)}), bf16[2048,1024]{1,0:T(8,128)(2,1)}) %all-gather.5.cloned.1.call-update) | async-done | bytes 4194320 | tf_op jit(solution)/shard_map/all_gather | solution.py:45
  726.1 4.6 copy.4
  (8 shorter events, 0.0 us)
Async XLA Ops:
  6.5 40.4 %all-gather.3.cloned.1.call-start = ((), (), s32[]{:S(2)}) async-start(), calls=%async_computation.1 | async-start | bytes 2621440 | tf_op jit(solution)/shard_map/all_gather | solution.py:25
  9.8 631.0 %reduce-scatter.2.cloned.1.call-start = ((), (), s32[]{:S(2)}) async-start(), calls=%async_computation.2 | async-start | bytes 8519680 | tf_op jit(solution)/shard_map/reduce_scatter | solution.py:38
  342.7 144.0 %copy-start = (bf16[1024,1024]{1,0:T(8,128)(2,1)S(1)}, bf16[1024,1024]{1,0:T(8,128)(2,1)}, u32[]{:S(2)}) copy-start(bf16[1024,1024]{1,0:T(8,128)(2,1)} %all-gather.3.cloned.1.call-done) | copy-start | bytes 6291460
  499.2 226.9 %all-gather.5.cloned.1.call-start = ((), (), s32[]{:S(2)}) async-start(), calls=%async_computation.3 | async-start | bytes 4259840 | tf_op jit(solution)/shard_map/all_gather | solution.py:45
Sparse Core Ops, SparseCore 0:
  9.9 36.9 all-gather.2
  499.3 141.4 reduce-scatter.1
  643.6 82.4 all-gather.4
where the time goes:
time: 738 us; the launch traced here: 737 us
  blocking collectives  407 us (55%)
  waiting for transfers between devices  261 us (35%)
  other arithmetic  27.7 us (4%)
  matrix products  23.1 us (3%)
  between operations  13.2 us (2%)
    psum x3, blocking collectives, column_total(): return lax.psum(partial_sum, 'dp')  387 us
    reduce_scatter x1, waiting for transfers between devices, per_device(): lax.psum_scatter(lax.dot_general(codes, group, (((0,), (0,)), ((), ())),...  142 us
    all_gather x1, waiting for transfers between devices, per_device(): lax.all_gather(rescaled.astype(jnp.bfloat16), 'dp', axis=0, tiled=True)  82.6 us
    all_gather x1, waiting for transfers between devices, per_device(): group = lax.all_gather(unit, 'proto', axis=0, tiled=True)  37.1 us
    psum x3, blocking collectives, row_total(): return lax.psum(partial_sum, 'proto')  20 us
  transfers between devices with their start and end apart: 3, of which 3 were waited for; matrix products, arithmetic and copies ran while one was open for 0% of the time, Pallas kernels for 0%

commit v1 on v0

--- a/solution.py
+++ b/solution.py
@@ -13,7 +13,7 @@
 
 
 def column_total(partial_sum):
-    return lax.psum(partial_sum, "dp")
+    return jnp.sum(lax.all_gather(partial_sum, "dp"), axis=0)
 
 
 def row_total(partial_sum):

time: 738 us -> 508 us (0.69)
  blocking collectives: 407 us -> 173 us
    psum x3 -> x0, blocking collectives: 387 us -> none  [column_total(): return lax.psum(partial_sum, 'dp')]
    all_gather x0 -> x3, blocking collectives: none -> 153 us  [column_total(): return jnp.sum(lax.all_gather(partial_sum, 'dp'), axis=0)]
where the time goes in v1:
time: 508 us
  waiting for transfers between devices  265 us (52%)
  blocking collectives  173 us (34%)
  other arithmetic  27.9 us (5%)
  matrix products  23.1 us (5%)
  between operations  13.2 us (3%)
    all_gather x3, blocking collectives, column_total(): return jnp.sum(lax.all_gather(partial_sum, 'dp'), axis=0)  153 us
    reduce_scatter x1, waiting for transfers between devices, per_device(): lax.psum_scatter(lax.dot_general(codes, group, (((0,), (0,)), ((), ())),...  146 us
    all_gather x1, waiting for transfers between devices, per_device(): lax.all_gather(rescaled.astype(jnp.bfloat16), 'dp', axis=0, tiled=True)  82.6 us
    all_gather x1, waiting for transfers between devices, per_device(): group = lax.all_gather(unit, 'proto', axis=0, tiled=True)  37.1 us
    psum x3, blocking collectives, row_total(): return lax.psum(partial_sum, 'proto')  20 us
    reduce_sum x3, other arithmetic, per_device(): rowsum = row_total(jnp.sum(plan, axis=1))  13 us
    dot_general x1, matrix products, per_device(): lax.dot_general(codes, group, (((0,), (0,)), ((), ())), preferred_element...  12.5 us
    dot_general x1, matrix products, per_device(): lax.dot_general(group, centres, (((1,), (1,)), ((), ())), preferred_eleme...  10.6 us
  transfers between devices with their start and end apart: 3, of which 3 were waited for; matrix products, arithmetic and copies ran while one was open for 0% of the time, Pallas kernels for 0%

profile of v1, /device:TPU:1, one launch (start us, length us, event | category | flops | bytes accessed | tf_op | source)
XLA Modules:
  0.0 508.1 jit_solution(13323348025492630326)
XLA Ops:
  6.5 0.0 all-gather.6.cloned.1.call-start
  6.5 1.2 fusion.15
  7.8 2.0 fusion.16
  9.8 0.0 all-gather.6.cloned.1.call-update
  9.8 0.0 reduce-scatter.2.cloned.1.call-start
  9.8 37.1 %all-gather.6.cloned.1.call-done = bf16[1024,1024]{1,0:T(8,128)(2,1)} async-done(((bf16[256,1024]{1,0:T(8,128)(2,1)}), bf16[1024,1024]{1,0:T(8,128)(2,1)}) %all-gather.6.cloned.1.call-update) | async-done | bytes 2097168 | tf_op jit(solution)/shard_map/all_gather | solution.py:25
  46.9 10.6 %fusion.18 = (f32[2048]{0:T(1024)S(1)}, f32[1024,2048]{1,0:T(8,128)}) fusion(bf16[1024,1024]{1,0:T(8,128)(2,1)} %all-gather.6.cloned.1.call-done, bf16[2048,1024]{1,0:T(8,128)(2,1)} %param.3), kind=kOutput, calls=%fused_computation.33 | convolution fusion | flops 4299159552 | bytes 14688256 | tf_op jit(solution)/shard_map/dot_general | solution.py:26
  57.5 51.9 %all-gather = f32[131072]{0:T(1024)S(1)} all-gather(f32[2048]{0:T(1024)S(1)} %get-tuple-element.5), channel_id=2, replica_groups=mesh['dp'=64,'proto'=4] {'dp'}, dimensions={0}, use_global_device_ids=true | all-gather | bytes 532480 | tf_op jit(solution)/shard_map/all_gather | solution.py:16
  109.4 0.1 reshape.28
  109.6 4.0 divide_reduce_fusion
  113.6 6.6 %psum.21 = f32[1024]{0:T(1024)S(1)} all-reduce(f32[1024]{0:T(1024)S(1)} %divide_reduce_fusion), channel_id=1, replica_groups=mesh['dp'=64,'proto'=4] {'proto'}, use_global_device_ids=true, to_apply=%region_4.0 | all-reduce | flops 1024 | bytes 8192 | tf_op jit(solution)/shard_map/psum | solution.py:20
  120.2 4.2 fusion.8
  124.3 51.0 %all-gather.1 = f32[131072]{0:T(1024)S(1)} all-gather(f32[2048]{0:T(1024)S(1)} %fusion.8), channel_id=3, replica_groups=mesh['dp'=64,'proto'=4] {'dp'}, dimensions={0}, use_global_device_ids=true | all-gather | bytes 532480 | tf_op jit(solution)/shard_map/all_gather | solution.py:16
  175.4 0.1 reshape.29
  175.5 4.4 fusion.10
  179.9 6.9 %psum.22 = f32[1024]{0:T(1024)S(1)} all-reduce(f32[1024]{0:T(1024)S(1)} %fusion.10), channel_id=1, replica_groups=mesh['dp'=64,'proto'=4] {'proto'}, use_global_device_ids=true, to_apply=%region_8.0 | all-reduce | flops 1024 | bytes 8192 | tf_op jit(solution)/shard_map/psum | solution.py:20
  186.8 0.0 copy-start
  186.8 4.6 fusion.11
  191.5 50.5 %all-gather.2 = f32[131072]{0:T(1024)S(1)} all-gather(f32[2048]{0:T(1024)S(1)} %fusion.11), channel_id=4, replica_groups=mesh['dp'=64,'proto'=4] {'dp'}, dimensions={0}, use_global_device_ids=true | all-gather | bytes 532480 | tf_op jit(solution)/shard_map/all_gather | solution.py:16
  242.0 0.1 reshape.30
  242.1 4.7 fusion.12
  246.8 6.6 %psum.23 = f32[1024]{0:T(1024)S(1)} all-reduce(f32[1024]{0:T(1024)S(1)} %fusion.12), channel_id=1, replica_groups=mesh['dp'=64,'proto'=4] {'proto'}, use_global_device_ids=true, to_apply=%region_12.0 | all-reduce | flops 1024 | bytes 8192 | tf_op jit(solution)/shard_map/psum | solution.py:20
  253.4 0.0 copy-done
  253.4 12.5 %fusion.13 = f32[2048,1024]{1,0:T(8,128)} fusion(bf16[1024,1024]{1,0:T(8,128)(2,1)S(1)} %copy-done, f32[1024,2048]{1,0:T(8,128)} %get-tuple-element.6, f32[1024]{0:T(1024)S(1)} %broadcast_multiply_fusion.3, f32[2048]{0:T(1024)S(1)} %broadcast_multiply_fusion, f32[1024]{0:T(1024)S(1)} %broadcast_multiply_fusion.4, f32[2048]{0:T(1024)S(1)} %broadcast_multiply_fusion.1, ...), kind=kOutput, calls=%fused_computation.17 | convolution fusion | flops 4311744512 | bytes 18911232 | tf_op jit(solution)/shard_map/dot_general | solution.py:39
  265.8 0.0 reduce-scatter.2.cloned.1.call-update
  265.9 0.0 all-gather.8.cloned.1.call-start
  265.9 145.7 %reduce-scatter.2.cloned.1.call-done = f32[32,1024]{1,0:T(8,128)} async-done(((f32[2048,1024]{1,0:T(8,128)}), f32[32,1024]{1,0:T(8,128)}) %reduce-scatter.2.cloned.1.call-update) | async-done | bytes 131088 | tf_op jit(solution)/shard_map/reduce_scatter | solution.py:38
  411.6 1.0 multiply_reduce_fusion
  412.6 1.6 multiply_convert_fusion
  414.2 0.0 all-gather.8.cloned.1.call-update
  414.2 82.6 %all-gather.8.cloned.1.call-done = bf16[2048,1024]{1,0:T(8,128)(2,1)} async-done(((bf16[32,1024]{1,0:T(8,128)(2,1)}), bf16[2048,1024]{1,0:T(8,128)(2,1)}) %all-gather.8.cloned.1.call-update) | async-done | bytes 4194320 | tf_op jit(solution)/shard_map/all_gather | solution.py:45
  496.9 4.6 copy.4
  (11 shorter events, 0.2 us)
Async XLA Ops:
  6.5 40.4 %all-gather.6.cloned.1.call-start = ((), (), s32[]{:S(2)}) async-start(), calls=%async_computation.1 | async-start | bytes 2621440 | tf_op jit(solution)/shard_map/all_gather | solution.py:25
  9.8 401.8 %reduce-scatter.2.cloned.1.call-start = ((), (), s32[]{:S(2)}) async-start(), calls=%async_computation.2 | async-start | bytes 8519680 | tf_op jit(solution)/shard_map/reduce_scatter | solution.py:38
  186.8 66.6 %copy-start = (bf16[1024,1024]{1,0:T(8,128)(2,1)S(1)}, bf16[1024,1024]{1,0:T(8,128)(2,1)}, u32[]{:S(2)}) copy-start(bf16[1024,1024]{1,0:T(8,128)(2,1)} %all-gather.6.cloned.1.call-done) | copy-start | bytes 6291460
  265.9 231.0 %all-gather.8.cloned.1.call-start = ((), (), s32[]{:S(2)}) async-start(), calls=%async_computation.3 | async-start | bytes 4259840 | tf_op jit(solution)/shard_map/all_gather | solution.py:45
Sparse Core Ops, SparseCore 0:
  9.9 36.9 all-gather.5
  266.0 145.5 reduce-scatter.1
  414.4 82.4 all-gather.7
